TPU v7x, 32 devices: a whole 2x2x4 slice. The times are simulated.
32 devices in a mesh: grp: 2 (over y), pair: 4 (over z), rep: 2 (over x), sub: 2 (over core).
Axes of the slice: x: 2, y: 2, z: 4, core: 2. Of those that a mesh axis runs over, the one named last changes fastest.
Arguments:
- cholesky: bfloat16 [256, 640, 640], P('sub', 'pair'), may hold values from -0.015625 to 0.015625
- trial_orbitals: bfloat16 [640, 192], replicated, may hold values from -0.25 to 0.25
- walkers: bfloat16 [32, 640, 192], P(('grp', 'pair', 'rep'), None, 'sub'), parts along dimension 0, may hold values from -6 to 6
- intersection_inverse: bfloat16 [32, 192, 192], P(('grp', 'pair', 'rep')), parts along dimension 0, may hold values from -0.4375 to 0.4375
- noise_stream: float32 [2048], P('grp'), parts along dimension 0, may hold values from -6 to 6
- offsets: int32 [32], P('grp'), parts along dimension 0, may hold values from 0 to 768
- parents: int32 [32], P(('grp', 'pair', 'rep')), parts along dimension 0, may hold values from 0 to 7
Outputs:
- new_walkers: bfloat16 [32, 640, 192], P(('grp', 'pair', 'rep'), None, 'sub'), parts along dimension 0
- force_bias: float32 [32, 256], P(('grp', 'pair', 'rep'), 'sub'), parts along dimension 0
There are 2 independent parts, one for each index of `grp`. A program takes and returns all parts, laid end to end along the dimension named above; an argument that names none is the same for every part. Nothing has to cross between parts.
All inputs are finite; a program needn't handle non-finite values.
Results may differ from a plain program's by a relative error of at most 0.035.
Values may be sent and summed in bfloat16 or wider, within the bound.
No kernel may reach another device: no remote copies, remote signals or barrier semaphores. Data moves between devices by JAX's collectives and lax.ppermute only.
A program may use at most 64 MiB of HBM per device.

v0:
```python
import jax
import jax.numpy as jnp
from jax import lax
from jax.sharding import PartitionSpec as P

TAYLOR = 6


field_scale = 1.6


def shards(cholesky, trial_orbitals, walkers, intersection_inverse, noise_stream, offsets, parents):
    chol_count = cholesky.shape[0]
    walk_count = walkers.shape[0]
    pair_size = lax.axis_size("pair")
    rep_size = lax.axis_size("rep")
    pair_index = lax.axis_index("pair")
    rep_index = lax.axis_index("rep")
    sub_index = lax.axis_index("sub")
    half_rotated = jnp.einsum(
        "gpq,qi->gpi", cholesky, trial_orbitals, preferred_element_type=jnp.float32
    ).astype(jnp.bfloat16)
    whole_walkers = lax.all_gather(walkers, "sub", axis=2, tiled=True)
    mixed = jnp.einsum(
        "wpj,wji->wpi", whole_walkers, intersection_inverse, preferred_element_type=jnp.float32
    ).astype(jnp.bfloat16)
    mixed_rows = lax.all_to_all(mixed, "pair", split_axis=1, concat_axis=0, tiled=True)
    partial_bias = jnp.einsum(
        "jpi,gpi->jg", mixed_rows, half_rotated, preferred_element_type=jnp.float32
    )
    window_start = sub_index * chol_count
    vector_steps = jnp.arange(chol_count, dtype=jnp.int32)

    def window_fields(offset_value, bias_row):
        drawn = noise_stream[offset_value + window_start + vector_steps]
        return (drawn - bias_row).astype(jnp.bfloat16)

    offsets_grid = offsets.reshape(pair_size, rep_size, walk_count)
    bias_totals = lax.psum(partial_bias.astype(jnp.bfloat16), "pair").astype(jnp.float32)
    row_offsets = lax.dynamic_index_in_dim(offsets_grid, rep_index, 1, False).reshape(-1)
    fields = jax.vmap(window_fields)(row_offsets, bias_totals)
    force_bias = lax.dynamic_slice_in_dim(bias_totals, pair_index * walk_count, walk_count, 0)
    partial_potential = jnp.einsum(
        "jg,gpq->jpq", fields, cholesky, preferred_element_type=jnp.float32
    )
    summed_potential = lax.psum(partial_potential.astype(jnp.bfloat16), "sub").astype(jnp.float32)
    potential = lax.all_to_all(
        (field_scale * summed_potential).astype(jnp.bfloat16),
        "pair",
        split_axis=0,
        concat_axis=1,
        tiled=True,
    )
    taylor_term = walkers
    summed = walkers.astype(jnp.float32)
    for degree in range(1, TAYLOR + 1):
        product = jnp.einsum(
            "wpq,wqi->wpi", potential, taylor_term, preferred_element_type=jnp.float32
        )
        taylor_term = (product / jnp.float32(degree)).astype(jnp.bfloat16)
        summed = summed + taylor_term.astype(jnp.float32)
    propagated = summed.astype(jnp.bfloat16)
    portion = lax.all_gather(propagated, "pair", axis=0, tiled=True)
    row_count = portion.shape[0]
    positions = jnp.arange(row_count, dtype=jnp.int32)
    selector = (parents[:, None] == positions[None, :]).astype(jnp.bfloat16)
    chosen = jnp.einsum("kr,rpi->kpi", selector, portion, preferred_element_type=jnp.float32)
    new_walkers = chosen.astype(jnp.bfloat16)
    return (new_walkers, force_bias)


def solution(mesh):
    in_specs = (
        P("sub", "pair", None),
        P(),
        P(("grp", "pair", "rep"), None, "sub"),
        P(("grp", "pair", "rep"), None, None),
        P("grp"),
        P("grp"),
        P(("grp", "pair", "rep")),
    )
    out_specs = (P(("grp", "pair", "rep"), None, "sub"), P(("grp", "pair", "rep"), "sub"))
    return jax.shard_map(shards, mesh=mesh, in_specs=in_specs, out_specs=out_specs, check_vma=False)
```

profile of v0, /device:TPU:0, one launch (start us, length us, event | category | flops | bytes accessed | tf_op | source)
XLA Modules:
  0.0 202.2 jit_solution(5442826918399444335)
XLA Ops:
  7.2 2.6 %all_gather.6 = bf16[2,640,192]{1,2,0:T(8,128)(2,1)S(1)} all-gather(bf16[2,640,96]{1,2,0:T(8,128)(2,1)} %param.9), channel_id=1, replica_groups=mesh['grp'=2,'pair'=4,'rep'=2,'sub'=2] {'sub'}, dimensions={2}, use_global_device_ids=true | all-gather | bytes 737280 | tf_op jit(solution)/shard_map/all_gather | solution.py:23
  9.8 1.3 convolution_convert_fusion
  11.1 1.8 copy.23
  12.9 6.2 %all-to-all-start = ((bf16[2,640,192]{2,0,1:T(2,128)(2,1)}), bf16[2,640,192]{2,0,1:T(2,128)(2,1)S(1)}, u32[]{:S(2)}, u32[]{:S(2)}) async-start(bf16[2,640,192]{2,0,1:T(2,128)(2,1)} %copy.23), calls=%async_computation | async-start | bytes 1310720 | tf_op jit(solution)/shard_map/all_to_all | solution.py:27
  19.4 4.5 %gather_fusion = f32[1024]{0:T(1024)S(1)} fusion(f32[1024]{0:T(1024)S(1)} %copy-done.1, s32[1024]{0:T(1024)S(1)} %fusion.35), kind=kCustom, calls=%fused_computation | custom fusion | bytes 12288 | tf_op jit(solution)/shard_map/vmap()/gather | solution.py:35
  24.0 12.8 %all-to-all-done = bf16[2,640,192]{2,0,1:T(2,128)(2,1)S(1)} async-done(((bf16[2,640,192]{2,0,1:T(2,128)(2,1)}), bf16[2,640,192]{2,0,1:T(2,128)(2,1)S(1)}, u32[]{:S(2)}, u32[]{:S(2)}) %all-to-all-start) | async-done | bytes 491552 | tf_op jit(solution)/shard_map/all_to_all | solution.py:27
  36.8 0.7 copy.25
  38.1 29.4 %fusion.26 = bf16[8,128]{1,0:T(8,128)(2,1)S(1)} fusion(bf16[8,160,192]{2,0,1:T(8,128)(2,1)S(1)} %all_to_all.29, bf16[128,160,640]{2,1,0:T(8,128)(2,1)} %param.7, bf16[640,192]{0,1:T(8,128)(2,1)S(1)} %copy-done), kind=kOutput, calls=%fused_computation.26 | convolution fusion | flops 5100012544 | bytes 26953728 | tf_op jit(solution)/shard_map/jpi,gpi->jg/dot_general | solution.py:28
  67.5 9.8 %psum.14 = bf16[8,128]{1,0:T(8,128)(2,1)S(1)} all-reduce(bf16[8,128]{1,0:T(8,128)(2,1)S(1)} %fusion.26), channel_id=1, replica_groups=mesh['grp'=2,'pair'=4,'rep'=2,'sub'=2] {'pair'}, use_global_device_ids=true, to_apply=%region_0.0 | all-reduce | flops 1024 | bytes 4096 | tf_op jit(solution)/shard_map/psum | solution.py:39
  77.4 26.5 %fusion.10 = bf16[8,160,640]{2,0,1:T(8,128)(2,1)} fusion(bf16[128,160,640]{2,1,0:T(8,128)(2,1)} %param.7, f32[1024]{0:T(1024)S(1)} %gather_fusion, bf16[8,128]{1,0:T(8,128)(2,1)S(1)} %psum.14), kind=kOutput, calls=%fused_computation.8 | convolution fusion | flops 210537472 | bytes 27858944 | tf_op jit(solution)/shard_map/jg,gpq->jpq/dot_general | solution.py:43
  103.8 18.9 %all-reduce.2.cloned.1.call-done = bf16[8,160,640]{2,0,1:T(8,128)(2,1)} async-done(((bf16[8,160,640]{2,0,1:T(8,128)(2,1)}), bf16[8,160,640]{2,0,1:T(8,128)(2,1)}) %all-reduce.2.cloned.1.call-update) | async-done | bytes 1638416 | tf_op jit(solution)/shard_map/psum | solution.py:46
  122.7 1.8 multiply_convert_fusion
  124.4 1.4 copy.28
  125.8 4.9 %all-to-all-start.1 = ((bf16[8,160,640]{2,1,0:T(8,128)(2,1)}), bf16[8,160,640]{2,1,0:T(8,128)(2,1)S(1)}, u32[]{:S(2)}, u32[]{:S(2)}) async-start(bf16[8,160,640]{2,1,0:T(8,128)(2,1)} %copy.28), calls=%async_computation.1 | async-start | bytes 3276800 | tf_op jit(solution)/shard_map/all_to_all | solution.py:47
  131.3 38.2 %all-to-all-done.1 = bf16[8,160,640]{2,1,0:T(8,128)(2,1)S(1)} async-done(((bf16[8,160,640]{2,1,0:T(8,128)(2,1)}), bf16[8,160,640]{2,1,0:T(8,128)(2,1)S(1)}, u32[]{:S(2)}, u32[]{:S(2)}) %all-to-all-start.1) | async-done | bytes 1638432 | tf_op jit(solution)/shard_map/all_to_all | solution.py:47
  169.7 0.8 copy-done.2
  170.5 0.6 convolution_convert_fusion.1
  171.1 0.6 fusion.13
  171.7 0.6 fusion.14
  172.3 0.6 fusion.15
  173.0 0.6 fusion.16
  173.6 0.7 fusion.20
  174.3 19.9 %all_gather.7 = bf16[8,640,96]{1,2,0:T(8,128)(2,1)S(1)} all-gather(bf16[2,640,96]{1,2,0:T(8,128)(2,1)S(1)} %fusion.20), channel_id=1, replica_groups=mesh['grp'=2,'pair'=4,'rep'=2,'sub'=2] {'pair'}, dimensions={0}, use_global_device_ids=true | all-gather | bytes 1228800 | tf_op jit(solution)/shard_map/all_gather | solution.py:63
  194.7 0.7 copy.31
  (21 shorter events, 2.3 us)
Async XLA Ops:
  7.2 31.0 %copy-start = (bf16[640,192]{0,1:T(8,128)(2,1)S(1)}, bf16[640,192]{0,1:T(8,128)(2,1)}, u32[]{:S(2)}) copy-start(bf16[640,192]{0,1:T(8,128)(2,1)} %param.8) | copy-start | bytes 737284
  9.8 9.3 %copy-start.4 = (s32[16]{0:T(128)S(1)}, s32[16]{0:T(128)}, u32[]{:S(2)}) copy-start(s32[16]{0:T(128)} %param.12) | copy-start | bytes 196
  9.8 9.6 %copy-start.1 = (f32[1024]{0:T(1024)S(1)}, f32[1024]{0:T(1024)}, u32[]{:S(2)}) copy-start(f32[1024]{0:T(1024)} %param.11) | copy-start | bytes 12292
  12.9 23.8 %all-to-all-start = ((bf16[2,640,192]{2,0,1:T(2,128)(2,1)}), bf16[2,640,192]{2,0,1:T(2,128)(2,1)S(1)}, u32[]{:S(2)}, u32[]{:S(2)}) async-start(bf16[2,640,192]{2,0,1:T(2,128)(2,1)} %copy.23), calls=%async_computation | async-start | bytes 1310720 | tf_op jit(solution)/shard_map/all_to_all | solution.py:27
  19.1 103.6 %all-reduce.2.cloned.1.call-start = ((), (), s32[]{:S(2)}) async-start(), calls=%async_computation.2 | async-start | bytes 3276800 | tf_op jit(solution)/shard_map/psum | solution.py:46
  125.8 43.7 %all-to-all-start.1 = ((bf16[8,160,640]{2,1,0:T(8,128)(2,1)}), bf16[8,160,640]{2,1,0:T(8,128)(2,1)S(1)}, u32[]{:S(2)}, u32[]{:S(2)}) async-start(bf16[8,160,640]{2,1,0:T(8,128)(2,1)} %copy.28), calls=%async_computation.1 | async-start | bytes 3276800 | tf_op jit(solution)/shard_map/all_to_all | solution.py:47
  169.5 0.9 copy-start.2
  173.6 20.5 %copy-start.3 = (s32[2]{0:T(128)S(1)}, s32[2]{0:T(128)}, u32[]{:S(2)}) copy-start(s32[2]{0:T(128)} %param.13) | copy-start | bytes 28
Sparse Core Ops, SparseCore 0:
  104.0 18.6 all-reduce.1
where the time goes:
time: 203 us; the launch traced here: 202 us
  waiting for transfers between devices  69.9 us (34%)
  matrix products  61.5 us (30%)
  blocking collectives  32.3 us (16%)
  between operations  14.1 us (7%)
  local copies, waits for them, and re-layouts  11.5 us (6%)
  starting transfers between devices  11.1 us (5%)
    all_to_all x1, waiting for transfers between devices, shards(): lax.all_to_all((field_scale * summed_potential).astype(jnp.bfloat16), 'pa...  38.2 us
    dot_general x1, matrix products, shards(): jnp.einsum('jpi,gpi->jg', mixed_rows, half_rotated, preferred_element_typ...  29.4 us
    dot_general x1, matrix products, shards(): jnp.einsum('jg,gpq->jpq', fields, cholesky, preferred_element_type=jnp.fl...  26.5 us
    all_gather x1, blocking collectives, shards(): portion = lax.all_gather(propagated, 'pair', axis=0, tiled=True)  19.9 us
    psum x1, waiting for transfers between devices, shards(): lax.psum(partial_potential.astype(jnp.bfloat16), 'sub').astype(jnp.float32)  18.9 us
    all_to_all x1, waiting for transfers between devices, shards(): lax.all_to_all(mixed, 'pair', split_axis=1, concat_axis=0, tiled=True)  12.8 us
    psum x1, blocking collectives, shards(): lax.psum(partial_bias.astype(jnp.bfloat16), 'pair').astype(jnp.float32)  9.83 us
    all_to_all x1, starting transfers between devices, shards(): lax.all_to_all(mixed, 'pair', split_axis=1, concat_axis=0, tiled=True)  6.23 us
  transfers between devices with their start and end apart: 3, of which 3 were waited for; matrix products, arithmetic and copies ran while one was open for 3% of the time, Pallas kernels for 0%

commit v1 on v0

--- a/solution.py
+++ b/solution.py
@@ -1,6 +1,10 @@
+import functools
+
 import jax
 import jax.numpy as jnp
 from jax import lax
+from jax.experimental import pallas as pl
+from jax.experimental.pallas import tpu as pltpu
 from jax.sharding import PartitionSpec as P
 
 TAYLOR = 6
@@ -8,8 +12,11 @@
 
 field_scale = 1.6
 
-
-def shards(cholesky, trial_orbitals, walkers, intersection_inverse, noise_stream, offsets, parents):
+LANES = 128
+STEP = 16
+
+
+def general_shards(cholesky, trial_orbitals, walkers, intersection_inverse, noise_stream, offsets, parents):
     chol_count = cholesky.shape[0]
     walk_count = walkers.shape[0]
     pair_size = lax.axis_size("pair")
@@ -69,6 +76,371 @@
     return (new_walkers, force_bias)
 
 
+VMEM = pl.BlockSpec(memory_space=pltpu.VMEM)
+SMEM = pl.BlockSpec(memory_space=pltpu.SMEM)
+HBM = pl.BlockSpec(memory_space=pltpu.HBM)
+f32 = jnp.float32
+bf16 = jnp.bfloat16
+
+
+def call(body, outs, in_specs, limit, flops, scratch=(), out_specs=None):
+    return pl.pallas_call(
+        body,
+        out_shape=outs,
+        in_specs=in_specs,
+        out_specs=out_specs if out_specs is not None else jax.tree.map(lambda _: VMEM, outs),
+        scratch_shapes=scratch,
+        compiler_params=pltpu.CompilerParams(vmem_limit_bytes=limit),
+        cost_estimate=pl.CostEstimate(flops=flops, bytes_accessed=1 << 16, transcendentals=0),
+        name=body.func.__name__ if isinstance(body, functools.partial) else body.__name__,
+    )
+
+
+def mix_kernel(n_pair, own_ref, other_ref, inverse_ref, *refs):
+    outs, whole = refs[:n_pair], refs[n_pair]
+    b, s = lax.axis_index("pair"), lax.axis_index("sub")
+    mine, theirs = own_ref[s], other_ref[s]
+    low = jnp.where(s == 0, mine, theirs)
+    high = jnp.where(s == 0, theirs, mine)
+    turned = jnp.concatenate([low, high], axis=0).astype(f32)
+    plain = turned.T.astype(bf16)
+    mixed = jnp.dot(plain, inverse_ref[s], preferred_element_type=f32).astype(bf16)
+    whole[...] = jnp.concatenate([mixed, plain], axis=1)
+    rows = outs[0].shape[0]
+    for x in range(n_pair):
+        outs[x][...] = whole[pl.ds(pl.multiple_of((b ^ x) * rows, STEP), rows), :]
+
+
+def rotate_kernel(n_pair, n_walk, chunk, chol_ref, trial_ref, noise_ref, offsets_ref, chol_out, half_out, spread_out, noise_out, sems):
+    n_tile, n_chol, rows, _ = chol_out.shape
+    copies = n_chol // chunk
+
+    def copy(c, j):
+        span = pl.ds(c * chunk, chunk)
+        return pltpu.make_async_copy(
+            chol_ref.at[span, :, pl.ds(j * LANES, LANES)], chol_out.at[j, span], sems.at[c, j]
+        )
+
+    for c in range(copies):
+        for j in range(n_tile):
+            copy(c, j).start()
+    b, r, s = lax.axis_index("pair"), lax.axis_index("rep"), lax.axis_index("sub")
+    n_rep = lax.axis_size("rep")
+    for y in range(n_pair):
+        for c in range(n_walk):
+            walker = ((b ^ y) * n_rep + r) * n_walk + (s ^ c)
+            start = offsets_ref[walker] + s * n_chol
+            line = start // LANES
+            shift = start - line * LANES
+            last = noise_ref.shape[0] - 1
+            pair = jnp.concatenate(
+                [noise_ref[pl.ds(line, 1), :], noise_ref[pl.ds(jnp.minimum(line + 1, last), 1), :]], axis=1
+            )
+            moved = pltpu.roll(jnp.broadcast_to(pair, (8, 2 * LANES)), 2 * LANES - shift, 1)
+            noise_out[pl.ds(y * n_walk + c, 1), :] = moved[:1, :LANES]
+    row = lax.broadcasted_iota(jnp.int32, spread_out.shape, 0)
+    lane = lax.broadcasted_iota(jnp.int32, spread_out.shape, 1)
+    spread_out[...] = jnp.where(lane // STEP == row, 1.0, 0.0).astype(bf16)
+    n_half, width = half_out.shape[0], trial_ref.shape[0]
+    trial = trial_ref[...]
+
+    def body(c, carry):
+        for j in range(n_tile):
+            copy(c, j).wait()
+        span = pl.ds(c * chunk, chunk)
+        block = jnp.concatenate([chol_out[j, span].reshape(chunk * rows, LANES) for j in range(n_tile)], axis=1)
+        rotated = lax.dot_general(block, trial, (((1,), (1,)), ((), ())), preferred_element_type=f32).astype(bf16)
+        if width < n_half * LANES:
+            rotated = jnp.concatenate([rotated, jnp.zeros((chunk * rows, n_half * LANES - width), bf16)], axis=1)
+        for h in range(n_half):
+            half_out[h, span] = rotated[:, h * LANES : (h + 1) * LANES].reshape(chunk, rows, LANES)
+        return carry
+
+    lax.fori_loop(0, copies, body, 0)
+
+
+def bias_kernel(n_el, own_ref, other_ref, half_ref, spread_ref, parents_ref, out_ref, left, lines):
+    n_pair, rows, _ = own_ref.shape
+    n_half, n_chol = half_ref.shape[0], half_ref.shape[1]
+    width = n_half * LANES
+    n_slot = 2 * n_pair
+    blocks = rows // STEP
+    for p in range(blocks):
+        span = slice(p * STEP, (p + 1) * STEP)
+        parts = [ref[y, span, :n_el] for y in range(n_pair) for ref in (own_ref, other_ref)]
+        block = jnp.concatenate(parts, axis=0)
+        if n_el < width:
+            block = jnp.concatenate([block, jnp.zeros((n_slot * STEP, width - n_el), bf16)], axis=1)
+        left[:, p * width : (p + 1) * width] = block
+    many = 2 * LANES // STEP
+    row = lax.broadcasted_iota(jnp.int32, (n_slot * STEP, 2 * LANES), 0)
+    lane = lax.broadcasted_iota(jnp.int32, (n_slot * STEP, 2 * LANES), 1)
+    same = row % STEP == lane % STEP
+
+    def body(c, carry):
+        span = pl.ds(c * many, many)
+        total = jnp.zeros((n_slot * STEP, 2 * LANES), f32)
+        for p in range(blocks):
+            right = jnp.concatenate(
+                [half_ref[h, span, p * STEP : (p + 1) * STEP, :].reshape(many * STEP, LANES) for h in range(n_half)], axis=1
+            )
+            total = total + lax.dot_general(
+                left[:, p * width : (p + 1) * width], right, (((1,), (1,)), ((), ())), preferred_element_type=f32
+            )
+        kept = jnp.where(same, total, 0.0).reshape(n_slot, STEP, 2 * LANES).sum(axis=1)
+        lines[:, pl.ds(pl.multiple_of(c * 2 * LANES, 2 * LANES), 2 * LANES)] = kept
+        return carry
+
+    lax.fori_loop(0, n_chol // many, body, 0)
+    rest = lines[...]
+    bias = jnp.zeros((n_slot, n_chol), f32)
+    for _ in range(3):
+        piece = rest.astype(bf16)
+        bias = bias + lax.dot_general(piece, spread_ref[...], (((1,), (1,)), ((), ())), preferred_element_type=f32)
+        rest = rest - piece.astype(f32)
+    out_ref[:n_slot, :] = bias
+    which = lax.broadcasted_iota(jnp.int32, (8, n_chol), 0)
+    out_ref[n_slot:, :] = jnp.where(which == 0, parents_ref[0], parents_ref[1]).astype(f32)
+
+
+def fields_kernel(n_pair, noise_ref, *refs):
+    biases, bias_out, fields_out, picks_out = refs[:n_pair], *refs[n_pair:]
+    b, s = lax.axis_index("pair"), lax.axis_index("sub")
+    n_slot = 2 * n_pair
+    total = biases[0][:n_slot, :]
+    for x in range(1, n_pair):
+        total = total + jnp.concatenate([biases[x][2 * (y ^ x) : 2 * (y ^ x) + 2, :] for y in range(n_pair)], axis=0)
+    bias_out[pl.ds(s, 1), :] = total[:1]
+    bias_out[pl.ds(1 - s, 1), :] = total[1:2]
+    walker_fields = (noise_ref[...] - total).astype(bf16).astype(f32)
+    ancestry = jnp.concatenate(
+        [biases[y][pl.ds(n_slot + (s ^ c), 1), :] for y in range(n_pair) for c in range(2)], axis=0
+    )
+    chosen = jnp.zeros_like(total)
+    for y in range(n_pair):
+        for c in range(2):
+            name = ((b ^ y) * 2 + (s ^ c)).astype(f32)
+            chosen = chosen + jnp.where(ancestry == name, walker_fields[2 * y + c : 2 * y + c + 1], 0.0)
+    fields_out[...] = chosen
+    slot_name = lax.broadcasted_iota(jnp.int32, ancestry.shape, 1)
+    mapped = ((slot_name // 2) ^ b) * 2 + ((slot_name % 2) ^ s)
+    picks_out[...] = jnp.where(ancestry == mapped.astype(f32), 1.0, 0.0)
+
+
+def potential_kernel(first, count, fields_ref, chol_ref, spread_ref, own_ref, send_ref, left):
+    n_tile, n_chol, rows, _ = chol_ref.shape
+    blocks = rows // STEP
+    width = n_chol * STEP
+    grown = jnp.dot(fields_ref[...].astype(bf16), spread_ref[...], preferred_element_type=f32)
+    row = lax.broadcasted_iota(jnp.int32, (STEP, width), 0)
+    lane = lax.broadcasted_iota(jnp.int32, (STEP, width), 1)
+    same = row == lane % STEP
+    for c in range(2):
+        for k in range(count):
+            slot = 2 * (first + k) + c
+            at = (c * count + k) * STEP
+            left[at : at + STEP, :] = jnp.where(same, jnp.broadcast_to(grown[slot : slot + 1], (STEP, width)), 0.0).astype(bf16)
+
+    def body(i, carry):
+        j = i // (blocks // 2)
+        p = (i - j * (blocks // 2)) * 2
+        spans = [pl.ds(pl.multiple_of((p + d) * STEP, STEP), STEP) for d in range(2)]
+        right = jnp.concatenate([chol_ref[j, :, span, :].reshape(width, LANES) for span in spans], axis=1)
+        product = jnp.dot(left[...], right, preferred_element_type=f32)
+        for k in range(count):
+            for d in range(2):
+                lanes = slice(d * LANES, (d + 1) * LANES)
+                own_ref[k, j, spans[d], :] = product[k * STEP : (k + 1) * STEP, lanes]
+                at = (count + k) * STEP
+                send_ref[k, j, spans[d], :] = product[at : at + STEP, lanes].astype(bf16)
+        return carry
+
+    lax.fori_loop(0, n_tile * (blocks // 2), body, 0)
+
+
+def join_kernel(first, n_el, own_ref, other_ref, picks_ref, mine_ref, theirs_ref, *outs):
+    n_pair = mine_ref.shape[0]
+    n_tile = own_ref.shape[1]
+    for k, out in enumerate(outs):
+        out[:n_tile] = (field_scale * (own_ref[k] + other_ref[k].astype(f32))).astype(bf16)
+        picked = jnp.zeros(mine_ref.shape[1:2] + (n_el,), f32)
+        for y in range(n_pair):
+            for c, ref in enumerate((mine_ref, theirs_ref)):
+                slot = 2 * y + c
+                weight = picks_ref[2 * (first + k) : 2 * (first + k) + 1, slot : slot + 1]
+                picked = picked + weight * ref[y, :, n_el : 2 * n_el].astype(f32)
+        picked = picked.astype(bf16)
+        for h in range(out.shape[0] - n_tile):
+            width = min(LANES, n_el - h * LANES)
+            out[n_tile + h, :, :width] = picked[:, h * LANES : h * LANES + width]
+
+
+def taylor_kernel(n_pair, n_tile, n_el, *refs):
+    blocks, keep_ref, send_ref, term, total = refs[:n_pair], *refs[n_pair:]
+    b, s = lax.axis_index("pair"), lax.axis_index("sub")
+    rows = blocks[0].shape[1]
+
+    def place(x):
+        return pl.ds(pl.multiple_of((b ^ x) * rows, STEP), rows)
+
+    n_half = blocks[0].shape[0] - n_tile
+    for x in range(n_pair):
+        start = jnp.concatenate(
+            [blocks[x][n_tile + h, :, : min(LANES, n_el - h * LANES)] for h in range(n_half)], axis=1
+        )
+        term[place(x), :] = start
+        total[x * rows : (x + 1) * rows, :] = start.astype(f32)
+    matrix = jnp.concatenate(
+        [jnp.concatenate([blocks[x][j] for j in range(n_tile)], axis=1) for x in range(n_pair)], axis=0
+    )
+    for degree in range(1, TAYLOR + 1):
+        product = jnp.dot(matrix, term[...], preferred_element_type=f32)
+        new = (product * f32(1.0 / degree)).astype(bf16)
+        total[...] += new.astype(f32)
+        if degree < TAYLOR:
+            for x in range(n_pair):
+                term[place(x), :] = new[x * rows : (x + 1) * rows]
+    for x in range(n_pair):
+        term[place(x), :] = total[x * rows : (x + 1) * rows, :].astype(bf16)
+    turned = term[...].astype(f32).T.astype(bf16)
+    half = n_el // 2
+    low, high = turned[:half], turned[half:]
+    keep_ref[...] = jnp.where(s == 0, low, high)
+    send_ref[...] = jnp.where(s == 0, high, low)
+
+
+def finish_kernel(keep_ref, other_ref, out_ref):
+    s = lax.axis_index("sub")
+    out_ref[s] = keep_ref[...]
+    out_ref[1 - s] = other_ref[...]
+
+
+def fast_shards(cholesky, trial_orbitals, walkers, intersection_inverse, noise_stream, offsets, parents):
+    n_chol, rows, n_orb = cholesky.shape
+    n_el = trial_orbitals.shape[1]
+    n_walk, _, half_el = walkers.shape
+    n_pair = lax.axis_size("pair")
+    n_tile = n_orb // LANES
+    n_half = pl.cdiv(n_el, LANES)
+    n_slot = n_pair * n_walk
+    chunk = 8
+
+    def across(value, x):
+        return lax.ppermute(value, "pair", [(i, i ^ x) for i in range(n_pair)])
+
+    def swap(value):
+        return lax.ppermute(value, "sub", [(0, 1), (1, 0)])
+
+    turned = jnp.swapaxes(walkers, 1, 2)
+    rows_out = call(
+        functools.partial(mix_kernel, n_pair),
+        [jax.ShapeDtypeStruct((rows, 2 * n_el), bf16)] * n_pair,
+        [VMEM] * 3,
+        8 << 20,
+        2 * n_orb * n_el * n_el,
+        [pltpu.VMEM((n_orb, 2 * n_el), bf16)],
+    )(turned, swap(turned), intersection_inverse)
+    arrived = [rows_out[0]] + [across(rows_out[x], x) for x in range(1, n_pair)]
+    resident, half_rotated, spread, noise = call(
+        functools.partial(rotate_kernel, n_pair, n_walk, chunk),
+        [
+            pltpu.VMEM((n_tile, n_chol, rows, LANES), bf16),
+            pltpu.VMEM((n_half, n_chol, rows, LANES), bf16),
+            pltpu.VMEM((n_chol, n_chol * STEP), bf16),
+            pltpu.VMEM((n_slot, n_chol), f32),
+        ],
+        [HBM, VMEM, VMEM, SMEM],
+        8 << 20,
+        2 * n_chol * rows * n_orb * n_el,
+        [pltpu.SemaphoreType.DMA((n_chol // chunk, n_tile))],
+    )(cholesky, trial_orbitals.T, noise_stream.reshape(-1, LANES), offsets)
+    mine = jnp.stack(arrived)
+    theirs = swap(mine)
+    partial_bias = call(
+        functools.partial(bias_kernel, n_el),
+        jax.ShapeDtypeStruct((n_slot + 8, n_chol), f32),
+        [VMEM] * 4 + [SMEM],
+        8 << 20,
+        2 * n_slot * STEP * n_chol * rows * n_el,
+        [
+            pltpu.VMEM((n_slot * STEP, rows // STEP * n_half * LANES), bf16),
+            pltpu.VMEM((n_slot, n_chol * STEP), f32),
+        ],
+    )(mine, theirs, half_rotated, spread, parents)
+    biases = [partial_bias] + [across(partial_bias, x) for x in range(1, n_pair)]
+    force_bias, fields, picks = call(
+        functools.partial(fields_kernel, n_pair),
+        [
+            jax.ShapeDtypeStruct((n_walk, n_chol), f32),
+            jax.ShapeDtypeStruct((n_slot, n_chol), f32),
+            jax.ShapeDtypeStruct((n_slot, n_chol), f32),
+        ],
+        [VMEM] * (1 + n_pair),
+        4 << 20,
+        1 << 10,
+    )(noise, *biases)
+    got = [None] * n_pair
+    half = n_pair // 2
+    for first in (half, 0):
+        own, send = call(
+            functools.partial(potential_kernel, first, half),
+            [
+                jax.ShapeDtypeStruct((half, n_tile, rows, LANES), f32),
+                jax.ShapeDtypeStruct((half, n_tile, rows, LANES), bf16),
+            ],
+            [VMEM] * 3,
+            8 << 20,
+            2 * n_pair * STEP * n_chol * rows * n_orb,
+            [pltpu.VMEM((n_pair * STEP, n_chol * STEP), bf16)],
+        )(fields, resident, spread)
+        joined = call(
+            functools.partial(join_kernel, first, n_el),
+            [jax.ShapeDtypeStruct((n_tile + n_half, rows, LANES), bf16)] * half,
+            [VMEM] * 5,
+            8 << 20,
+            1 << 10,
+        )(own, swap(send), picks, mine, theirs)
+        for k in range(half):
+            x = first + k
+            got[x] = across(joined[k], x) if x else joined[k]
+    keep, give = call(
+        functools.partial(taylor_kernel, n_pair, n_tile, n_el),
+        [jax.ShapeDtypeStruct((half_el, n_orb), bf16)] * 2,
+        [VMEM] * n_pair,
+        16 << 20,
+        2 * TAYLOR * n_orb * n_orb * n_el,
+        [pltpu.VMEM((n_orb, n_el), bf16), pltpu.VMEM((n_orb, n_el), f32)],
+    )(*got)
+    new_turned = call(
+        finish_kernel,
+        jax.ShapeDtypeStruct((n_walk, half_el, n_orb), bf16),
+        [VMEM] * 2,
+        4 << 20,
+        1 << 10,
+    )(keep, swap(give))
+    return (jnp.swapaxes(new_turned, 1, 2), force_bias)
+
+
+def fits(mesh, cholesky, trial_orbitals, walkers, noise_stream):
+    sizes = mesh.shape
+    n_pair, n_sub = sizes["pair"], sizes["sub"]
+    rows = cholesky.shape[1] // n_pair
+    n_chol = cholesky.shape[0] // n_sub
+    n_walk = walkers.shape[0] // (sizes["grp"] * n_pair * sizes["rep"])
+    resident = n_chol * rows * (cholesky.shape[2] + 2 * LANES) * 2
+    return (
+        n_sub == 2
+        and n_walk == 2
+        and n_pair in (2, 4)
+        and rows % (2 * STEP) == 0
+        and cholesky.shape[2] % LANES == 0
+        and n_chol == LANES
+        and trial_orbitals.shape[1] <= 2 * LANES
+        and noise_stream.shape[0] // sizes["grp"] % LANES == 0
+        and resident <= 40 << 20
+    )
+
+
 def solution(mesh):
     in_specs = (
         P("sub", "pair", None),
@@ -80,4 +452,11 @@
         P(("grp", "pair", "rep")),
     )
     out_specs = (P(("grp", "pair", "rep"), None, "sub"), P(("grp", "pair", "rep"), "sub"))
-    return jax.shard_map(shards, mesh=mesh, in_specs=in_specs, out_specs=out_specs, check_vma=False)
+
+    def step(cholesky, trial_orbitals, walkers, intersection_inverse, noise_stream, offsets, parents):
+        body = fast_shards if fits(mesh, cholesky, trial_orbitals, walkers, noise_stream) else general_shards
+        return jax.shard_map(body, mesh=mesh, in_specs=in_specs, out_specs=out_specs, check_vma=False)(
+            cholesky, trial_orbitals, walkers, intersection_inverse, noise_stream, offsets, parents
+        )
+
+    return step

time: 203 us -> 117 us (0.58)
  the two profiles are of different devices: /device:TPU:0 before, /device:TPU:17 now
where the time goes in v1:
time: 117 us
  Pallas kernels  43 us (37%)
  waiting for transfers between devices  38.6 us (33%)
  local copies, waits for them, and re-layouts  21.3 us (18%)
  starting transfers between devices  13.5 us (12%)
    ppermute x9, waiting for transfers between devices, across(): return lax.ppermute(value, 'pair', [(i, i ^ x) for i in range(n_pair)])  36.2 us
    unnamed x16, local copies, waits for them, and re-layouts  21.3 us
    pallas_call x2, Pallas kernels, fast_shards(): call(functools.partial(potential_kernel, first, half), [jax.ShapeDtypeStr...  16.1 us
    pallas_call x1, Pallas kernels, fast_shards(): call(functools.partial(rotate_kernel, n_pair, n_walk, chunk), [pltpu.VMEM...  14.3 us
    ppermute x9, starting transfers between devices, across(): return lax.ppermute(value, 'pair', [(i, i ^ x) for i in range(n_pair)])  9.06 us
    pallas_call x1, Pallas kernels, fast_shards(): call(functools.partial(bias_kernel, n_el), jax.ShapeDtypeStruct((n_slot +...  5.63 us
    ppermute x5, starting transfers between devices, swap(): return lax.ppermute(value, 'sub', [(0, 1), (1, 0)])  4.48 us
    pallas_call x1, Pallas kernels, fast_shards(): call(functools.partial(taylor_kernel, n_pair, n_tile, n_el), [jax.ShapeDt...  4.24 us
  transfers between devices with their start and end apart: 14, of which 9 were waited for; matrix products, arithmetic and copies ran while one was open for 0% of the time, Pallas kernels for 20%

profile of v1, /device:TPU:17, one launch (start us, length us, event | category | flops | bytes accessed | tf_op | source)
XLA Modules:
  0.0 117.2 jit_solution(12682347870534739581)
XLA Ops:
  1.4 1.3 %collective-permute-done.other_ref = bf16[2,96,640]{2,1,0:T(8,128)(2,1)S(1)} collective-permute-done((bf16[2,96,640]{2,1,0:T(8,128)(2,1)}, bf16[2,96,640]{2,1,0:T(8,128)(2,1)S(1)}, u32[]{:S(2)}, u32[]{:S(2)}) %collective-permute-start) | collective-permute-done | bytes 245792 | tf_op jit(solution)/shard_map/ppermute | solution.py:332
  2.7 0.9 copy-done.2
  5.0 1.4 %collective-permute-start.1 = (bf16[160,384]{1,0:T(8,128)(2,1)S(1)}, bf16[160,384]{1,0:T(8,128)(2,1)S(1)}, u32[]{:S(2)}, u32[]{:S(2)}) collective-permute-start(bf16[160,384]{1,0:T(8,128)(2,1)S(1)} %get-tuple-element.25), channel_id=1, source_target_pairs={{0,4},{4,0},{8,12},{12,8},{1,5},{5,1},{9,13},{13,9},{2,6},{6,2},{1... | collective-permute-start | bytes 368648 | tf_op jit(solution)/shard_map/ppermute | solution.py:329
  6.4 1.3 %collective-permute-start.3 = (bf16[160,384]{1,0:T(8,128)(2,1)S(1)}, bf16[160,384]{1,0:T(8,128)(2,1)S(1)}, u32[]{:S(2)}, u32[]{:S(2)}) collective-permute-start(bf16[160,384]{1,0:T(8,128)(2,1)S(1)} %get-tuple-element.27), channel_id=1, source_target_pairs={{0,12},{4,8},{8,4},{12,0},{1,13},{5,9},{9,5},{13,1},{2,14},{6,10},... | collective-permute-start | bytes 368648 | tf_op jit(solution)/shard_map/ppermute | solution.py:329
  7.7 2.2 %collective-permute-done.1 = bf16[160,384]{1,0:T(8,128)(2,1)S(1)} collective-permute-done((bf16[160,384]{1,0:T(8,128)(2,1)S(1)}, bf16[160,384]{1,0:T(8,128)(2,1)S(1)}, u32[]{:S(2)}, u32[]{:S(2)}) %collective-permute-start.1) | collective-permute-done | bytes 122912 | tf_op jit(solution)/shard_map/ppermute | solution.py:329
  9.9 2.2 %collective-permute-done.2 = bf16[160,384]{1,0:T(8,128)(2,1)S(1)} collective-permute-done((bf16[160,384]{1,0:T(8,128)(2,1)S(1)}, bf16[160,384]{1,0:T(8,128)(2,1)S(1)}, u32[]{:S(2)}, u32[]{:S(2)}) %collective-permute-start.2) | collective-permute-done | bytes 122912 | tf_op jit(solution)/shard_map/ppermute | solution.py:329
  12.1 6.4 %collective-permute-done.3 = bf16[160,384]{1,0:T(8,128)(2,1)S(1)} collective-permute-done((bf16[160,384]{1,0:T(8,128)(2,1)S(1)}, bf16[160,384]{1,0:T(8,128)(2,1)S(1)}, u32[]{:S(2)}, u32[]{:S(2)}) %collective-permute-start.3) | collective-permute-done | bytes 122912 | tf_op jit(solution)/shard_map/ppermute | solution.py:329
  18.6 1.5 %collective-permute-start.4 = (bf16[4,160,384]{2,1,0:T(8,128)(2,1)S(1)}, bf16[4,160,384]{2,1,0:T(8,128)(2,1)S(1)}, u32[]{:S(2)}, u32[]{:S(2)}) collective-permute-start(bf16[4,160,384]{2,1,0:T(8,128)(2,1)S(1)} %pad_maximum_fusion.own_ref.mine_ref), channel_id=1, source_target_pairs={{0,1},{1,0},{2,3},{3,2},{4,5},{5,4},{6,7},{7,6},{8,9},{9,8},{10,11... | collective-permute-start | bytes 1474568 | tf_op jit(solution)/shard_map/ppermute | solution.py:332
  22.4 14.3 %rotate_kernel.1 = (bf16[5,128,160,128]{3,2,1,0:T(8,128)(2,1)S(1)}, bf16[2,128,160,128]{3,2,1,0:T(8,128)(2,1)S(1)}, bf16[128,2048]{1,0:T(8,128)(2,1)S(1)}, f32[8,128]{1,0:T(8,128)S(1)}) custom-call(bf16[128,160,640]{2,1,0:T(8,128)(2,1)} %chol_ref.1, bf16[192,640]{1,0:T(8,128)(2,1)S(1)} %bitcast.10, f32[8,128]{1,0:T(8,128)S(1)} %bitcast.12, s32[16]{0:T(128)S(1)} %copy-done.6), custom_call_target="tpu_custom_call" | custom-call | flops 5033164800 | bytes 65536 | tf_op jit(solution)/shard_map/rotate_kernel/pallas_call | solution.py:344
  36.7 8.7 %copy-done = bf16[5,128,160,128]{3,2,1,0:T(8,128)(2,1)} copy-done((bf16[5,128,160,128]{3,2,1,0:T(8,128)(2,1)}, bf16[5,128,160,128]{3,2,1,0:T(8,128)(2,1)S(1)}, u32[]{:S(2)}) %copy-start) | copy-done | bytes 26214424
  45.3 5.6 %bias_kernel.1.refs_0_ = f32[16,128]{1,0:T(8,128)S(1)} custom-call(bf16[4,160,384]{2,1,0:T(8,128)(2,1)S(1)} %pad_maximum_fusion.own_ref.mine_ref, bf16[4,160,384]{2,1,0:T(8,128)(2,1)S(1)} %collective-permute-done.4.other_ref.theirs_ref, bf16[2,128,160,128]{3,2,1,0:T(8,128)(2,1)S(1)} %get-tuple-element.28.half_ref, ...), custom_call_target="tpu_custom_call" | custom-call | flops 1006632960 | bytes 65536 | tf_op jit(solution)/shard_map/bias_kernel/pallas_call | solution.py:359
  51.2 1.4 %collective-permute-start.6 = (f32[16,128]{1,0:T(8,128)S(1)}, f32[16,128]{1,0:T(8,128)S(1)}, u32[]{:S(2)}, u32[]{:S(2)}) collective-permute-start(f32[16,128]{1,0:T(8,128)S(1)} %bias_kernel.1.refs_0_), channel_id=1, source_target_pairs={{0,8},{4,12},{8,0},{12,4},{1,9},{5,13},{9,1},{13,5},{2,10},{6,14},... | collective-permute-start | bytes 24584 | tf_op jit(solution)/shard_map/ppermute | solution.py:329
  52.6 1.1 collective-permute-start.5
  53.6 1.0 collective-permute-done.6.refs_2_
  55.9 8.5 %copy-done.1 = bf16[5,128,160,128]{3,2,1,0:T(8,128)(2,1)S(1)} copy-done((bf16[5,128,160,128]{3,2,1,0:T(8,128)(2,1)S(1)}, bf16[5,128,160,128]{3,2,1,0:T(8,128)(2,1)}, u32[]{:S(2)}) %copy-start.1) | copy-done | bytes 26214424
  64.4 8.0 %potential_kernel.3 = (f32[2,5,160,128]{3,2,1,0:T(8,128)S(1)}, bf16[2,5,160,128]{3,2,1,0:T(8,128)(2,1)S(1)}) custom-call(f32[8,128]{1,0:T(8,128)S(1)} %get-tuple-element.30.fields_ref, bf16[5,128,160,128]{3,2,1,0:T(8,128)(2,1)S(1)} %copy-done.1, bf16[128,2048]{1,0:T(8,128)(2,1)S(1)} %get-tuple-element.29.spread_ref), custom_call_target="tpu_custom_call" | custom-call | flops 1677721600 | bytes 65536 | tf_op jit(solution)/shard_map/potential_kernel/pallas_call | solution.py:385
  72.4 1.5 %collective-permute-start.10 = (bf16[2,5,160,128]{3,2,1,0:T(8,128)(2,1)S(1)}, bf16[2,5,160,128]{3,2,1,0:T(8,128)(2,1)S(1)}, u32[]{:S(2)}, u32[]{:S(2)}) collective-permute-start(bf16[2,5,160,128]{3,2,1,0:T(8,128)(2,1)S(1)} %get-tuple-element.38), channel_id=1, source_target_pairs={{0,1},{1,0},{2,3},{3,2},{4,5},{5,4},{6,7},{7,6},{8,9},{9,8},{10,11... | collective-permute-start | bytes 1228808 | tf_op jit(solution)/shard_map/ppermute | solution.py:332
  73.9 8.0 %potential_kernel.2 = (f32[2,5,160,128]{3,2,1,0:T(8,128)S(1)}, bf16[2,5,160,128]{3,2,1,0:T(8,128)(2,1)S(1)}) custom-call(f32[8,128]{1,0:T(8,128)S(1)} %get-tuple-element.30.fields_ref, bf16[5,128,160,128]{3,2,1,0:T(8,128)(2,1)S(1)} %copy-done.1, bf16[128,2048]{1,0:T(8,128)(2,1)S(1)} %get-tuple-element.29.spread_ref), custom_call_target="tpu_custom_call" | custom-call | flops 1677721600 | bytes 65536 | tf_op jit(solution)/shard_map/potential_kernel/pallas_call | solution.py:385
  83.5 1.4 %collective-permute-start.12 = (bf16[7,160,128]{2,1,0:T(8,128)(2,1)S(1)}, bf16[7,160,128]{2,1,0:T(8,128)(2,1)S(1)}, u32[]{:S(2)}, u32[]{:S(2)}) collective-permute-start(bf16[7,160,128]{2,1,0:T(8,128)(2,1)S(1)} %get-tuple-element.40), channel_id=1, source_target_pairs={{0,12},{4,8},{8,4},{12,0},{1,13},{5,9},{9,5},{13,1},{2,14},{6,10},... | collective-permute-start | bytes 860168 | tf_op jit(solution)/shard_map/ppermute | solution.py:329
  85.5 1.4 %collective-permute-start.9 = (bf16[7,160,128]{2,1,0:T(8,128)(2,1)S(1)}, bf16[7,160,128]{2,1,0:T(8,128)(2,1)S(1)}, u32[]{:S(2)}, u32[]{:S(2)}) collective-permute-start(bf16[7,160,128]{2,1,0:T(8,128)(2,1)S(1)} %get-tuple-element.36), channel_id=1, source_target_pairs={{0,4},{4,0},{8,12},{12,8},{1,5},{5,1},{9,13},{13,9},{2,6},{6,2},{1... | collective-permute-start | bytes 860168 | tf_op jit(solution)/shard_map/ppermute | solution.py:329
  86.9 15.0 %collective-permute-done.11.refs_2_ = bf16[7,160,128]{2,1,0:T(8,128)(2,1)S(1)} collective-permute-done((bf16[7,160,128]{2,1,0:T(8,128)(2,1)S(1)}, bf16[7,160,128]{2,1,0:T(8,128)(2,1)S(1)}, u32[]{:S(2)}, u32[]{:S(2)}) %collective-permute-start.11) | collective-permute-done | bytes 286752 | tf_op jit(solution)/shard_map/ppermute | solution.py:329
  101.9 8.7 %collective-permute-done.12.refs_3_ = bf16[7,160,128]{2,1,0:T(8,128)(2,1)S(1)} collective-permute-done((bf16[7,160,128]{2,1,0:T(8,128)(2,1)S(1)}, bf16[7,160,128]{2,1,0:T(8,128)(2,1)S(1)}, u32[]{:S(2)}, u32[]{:S(2)}) %collective-permute-start.12) | collective-permute-done | bytes 286752 | tf_op jit(solution)/shard_map/ppermute | solution.py:329
  110.6 4.2 %taylor_kernel.1 = (bf16[96,640]{1,0:T(8,128)(2,1)S(1)}, bf16[96,640]{1,0:T(8,128)(2,1)S(1)}) custom-call(bf16[7,160,128]{2,1,0:T(8,128)(2,1)S(1)} %get-tuple-element.35.refs_0_, bf16[7,160,128]{2,1,0:T(8,128)(2,1)S(1)} %collective-permute-done.9.refs_1_, bf16[7,160,128]{2,1,0:T(8,128)(2,1)S(1)} %collective-permute-done.11.refs_2_, ...), custom_call_target="tpu_custom_call" | custom-call | flops 943718400 | bytes 65536 | tf_op jit(solution)/shard_map/taylor_kernel/pallas_call | solution.py:406
  115.5 1.0 collective-permute-done.13.other_ref
  (31 shorter events, 9.5 us)
Async XLA Ops:
  0.6 44.7 %copy-start.7 = (s32[2]{0:T(128)S(1)}, s32[2]{0:T(128)}, u32[]{:S(2)}) copy-start(s32[2]{0:T(128)} %parents_ref.1) | copy-start | bytes 28
  0.6 2.1 %collective-permute-start = (bf16[2,96,640]{2,1,0:T(8,128)(2,1)}, bf16[2,96,640]{2,1,0:T(8,128)(2,1)S(1)}, u32[]{:S(2)}, u32[]{:S(2)}) collective-permute-start(bf16[2,96,640]{2,1,0:T(8,128)(2,1)} %bitcast.8), channel_id=1, source_target_pairs={{0,1},{1,0},{2,3},{3,2},{4,5},{5,4},{6,7},{7,6},{8,9},{9,8},{10,11... | collective-permute-start | bytes 737288 | tf_op jit(solution)/shard_map/ppermute | solution.py:332
  2.7 0.9 copy-start.2
  3.7 0.9 copy-start.4
  5.0 5.0 %collective-permute-start.1 = (bf16[160,384]{1,0:T(8,128)(2,1)S(1)}, bf16[160,384]{1,0:T(8,128)(2,1)S(1)}, u32[]{:S(2)}, u32[]{:S(2)}) collective-permute-start(bf16[160,384]{1,0:T(8,128)(2,1)S(1)} %get-tuple-element.25), channel_id=1, source_target_pairs={{0,4},{4,0},{8,12},{12,8},{1,5},{5,1},{9,13},{13,9},{2,6},{6,2},{1... | collective-permute-start | bytes 368648 | tf_op jit(solution)/shard_map/ppermute | solution.py:329
  6.4 5.7 %collective-permute-start.2 = (bf16[160,384]{1,0:T(8,128)(2,1)S(1)}, bf16[160,384]{1,0:T(8,128)(2,1)S(1)}, u32[]{:S(2)}, u32[]{:S(2)}) collective-permute-start(bf16[160,384]{1,0:T(8,128)(2,1)S(1)} %get-tuple-element.26), channel_id=1, source_target_pairs={{0,8},{4,12},{8,0},{12,4},{1,9},{5,13},{9,1},{13,5},{2,10},{6,14},... | collective-permute-start | bytes 368648 | tf_op jit(solution)/shard_map/ppermute | solution.py:329
  6.4 12.1 %collective-permute-start.3 = (bf16[160,384]{1,0:T(8,128)(2,1)S(1)}, bf16[160,384]{1,0:T(8,128)(2,1)S(1)}, u32[]{:S(2)}, u32[]{:S(2)}) collective-permute-start(bf16[160,384]{1,0:T(8,128)(2,1)S(1)} %get-tuple-element.27), channel_id=1, source_target_pairs={{0,12},{4,8},{8,4},{12,0},{1,13},{5,9},{9,5},{13,1},{2,14},{6,10},... | collective-permute-start | bytes 368648 | tf_op jit(solution)/shard_map/ppermute | solution.py:329
  18.6 26.8 %collective-permute-start.4 = (bf16[4,160,384]{2,1,0:T(8,128)(2,1)S(1)}, bf16[4,160,384]{2,1,0:T(8,128)(2,1)S(1)}, u32[]{:S(2)}, u32[]{:S(2)}) collective-permute-start(bf16[4,160,384]{2,1,0:T(8,128)(2,1)S(1)} %pad_maximum_fusion.own_ref.mine_ref), channel_id=1, source_target_pairs={{0,1},{1,0},{2,3},{3,2},{4,5},{5,4},{6,7},{7,6},{8,9},{9,8},{10,11... | collective-permute-start | bytes 1474568 | tf_op jit(solution)/shard_map/ppermute | solution.py:332
  20.1 0.9 copy-start.3
  21.0 0.7 copy-start.5
  21.7 0.7 copy-start.6
  36.7 8.7 %copy-start = (bf16[5,128,160,128]{3,2,1,0:T(8,128)(2,1)}, bf16[5,128,160,128]{3,2,1,0:T(8,128)(2,1)S(1)}, u32[]{:S(2)}) copy-start(bf16[5,128,160,128]{3,2,1,0:T(8,128)(2,1)S(1)} %get-tuple-element.31.chol_ref) | copy-start | bytes 78643200
  51.0 2.7 %collective-permute-start.7 = (f32[16,128]{1,0:T(8,128)S(1)}, f32[16,128]{1,0:T(8,128)S(1)}, u32[]{:S(2)}, u32[]{:S(2)}) collective-permute-start(f32[16,128]{1,0:T(8,128)S(1)} %bias_kernel.1.refs_0_), channel_id=1, source_target_pairs={{0,12},{4,8},{8,4},{12,0},{1,13},{5,9},{9,5},{13,1},{2,14},{6,10},... | collective-permute-start | bytes 24584 | tf_op jit(solution)/shard_map/ppermute | solution.py:329
  51.2 3.5 %collective-permute-start.6 = (f32[16,128]{1,0:T(8,128)S(1)}, f32[16,128]{1,0:T(8,128)S(1)}, u32[]{:S(2)}, u32[]{:S(2)}) collective-permute-start(f32[16,128]{1,0:T(8,128)S(1)} %bias_kernel.1.refs_0_), channel_id=1, source_target_pairs={{0,8},{4,12},{8,0},{12,4},{1,9},{5,13},{9,1},{13,5},{2,10},{6,14},... | collective-permute-start | bytes 24584 | tf_op jit(solution)/shard_map/ppermute | solution.py:329
  52.6 2.8 %collective-permute-start.5 = (f32[16,128]{1,0:T(8,128)S(1)}, f32[16,128]{1,0:T(8,128)S(1)}, u32[]{:S(2)}, u32[]{:S(2)}) collective-permute-start(f32[16,128]{1,0:T(8,128)S(1)} %bias_kernel.1.refs_0_), channel_id=1, source_target_pairs={{0,4},{4,0},{8,12},{12,8},{1,5},{5,1},{9,13},{13,9},{2,6},{6,2},{1... | collective-permute-start | bytes 24584 | tf_op jit(solution)/shard_map/ppermute | solution.py:329
  55.9 8.5 %copy-start.1 = (bf16[5,128,160,128]{3,2,1,0:T(8,128)(2,1)S(1)}, bf16[5,128,160,128]{3,2,1,0:T(8,128)(2,1)}, u32[]{:S(2)}) copy-start(bf16[5,128,160,128]{3,2,1,0:T(8,128)(2,1)} %copy-done) | copy-start | bytes 78643200
  72.4 9.6 %collective-permute-start.10 = (bf16[2,5,160,128]{3,2,1,0:T(8,128)(2,1)S(1)}, bf16[2,5,160,128]{3,2,1,0:T(8,128)(2,1)S(1)}, u32[]{:S(2)}, u32[]{:S(2)}) collective-permute-start(bf16[2,5,160,128]{3,2,1,0:T(8,128)(2,1)S(1)} %get-tuple-element.38), channel_id=1, source_target_pairs={{0,1},{1,0},{2,3},{3,2},{4,5},{5,4},{6,7},{7,6},{8,9},{9,8},{10,11... | collective-permute-start | bytes 1228808 | tf_op jit(solution)/shard_map/ppermute | solution.py:332
  82.0 3.0 %collective-permute-start.8 = (bf16[2,5,160,128]{3,2,1,0:T(8,128)(2,1)S(1)}, bf16[2,5,160,128]{3,2,1,0:T(8,128)(2,1)S(1)}, u32[]{:S(2)}, u32[]{:S(2)}) collective-permute-start(bf16[2,5,160,128]{3,2,1,0:T(8,128)(2,1)S(1)} %get-tuple-element.33), channel_id=1, source_target_pairs={{0,1},{1,0},{2,3},{3,2},{4,5},{5,4},{6,7},{7,6},{8,9},{9,8},{10,11... | collective-permute-start | bytes 1228808 | tf_op jit(solution)/shard_map/ppermute | solution.py:332
  82.6 19.2 %collective-permute-start.11 = (bf16[7,160,128]{2,1,0:T(8,128)(2,1)S(1)}, bf16[7,160,128]{2,1,0:T(8,128)(2,1)S(1)}, u32[]{:S(2)}, u32[]{:S(2)}) collective-permute-start(bf16[7,160,128]{2,1,0:T(8,128)(2,1)S(1)} %get-tuple-element.39), channel_id=1, source_target_pairs={{0,8},{4,12},{8,0},{12,4},{1,9},{5,13},{9,1},{13,5},{2,10},{6,14},... | collective-permute-start | bytes 860168 | tf_op jit(solution)/shard_map/ppermute | solution.py:329
  83.5 27.1 %collective-permute-start.12 = (bf16[7,160,128]{2,1,0:T(8,128)(2,1)S(1)}, bf16[7,160,128]{2,1,0:T(8,128)(2,1)S(1)}, u32[]{:S(2)}, u32[]{:S(2)}) collective-permute-start(bf16[7,160,128]{2,1,0:T(8,128)(2,1)S(1)} %get-tuple-element.40), channel_id=1, source_target_pairs={{0,12},{4,8},{8,4},{12,0},{1,13},{5,9},{9,5},{13,1},{2,14},{6,10},... | collective-permute-start | bytes 860168 | tf_op jit(solution)/shard_map/ppermute | solution.py:329
  85.5 25.1 %collective-permute-start.9 = (bf16[7,160,128]{2,1,0:T(8,128)(2,1)S(1)}, bf16[7,160,128]{2,1,0:T(8,128)(2,1)S(1)}, u32[]{:S(2)}, u32[]{:S(2)}) collective-permute-start(bf16[7,160,128]{2,1,0:T(8,128)(2,1)S(1)} %get-tuple-element.36), channel_id=1, source_target_pairs={{0,4},{4,0},{8,12},{12,8},{1,5},{5,1},{9,13},{13,9},{2,6},{6,2},{1... | collective-permute-start | bytes 860168 | tf_op jit(solution)/shard_map/ppermute | solution.py:329
  114.8 1.7 %collective-permute-start.13 = (bf16[96,640]{1,0:T(8,128)(2,1)S(1)}, bf16[96,640]{1,0:T(8,128)(2,1)S(1)}, u32[]{:S(2)}, u32[]{:S(2)}) collective-permute-start(bf16[96,640]{1,0:T(8,128)(2,1)S(1)} %get-tuple-element.42), channel_id=1, source_target_pairs={{0,1},{1,0},{2,3},{3,2},{4,5},{5,4},{6,7},{7,6},{8,9},{9,8},{10,11... | collective-permute-start | bytes 368648 | tf_op jit(solution)/shard_map/ppermute | solution.py:332
